TPU v7x, 32 devices: a whole 2x2x4 slice. The times are simulated.
32 devices in a mesh: au: 8 (over z, core), vert: 4 (over y, x).
Axes of the slice: x: 2, y: 2, z: 4, core: 2. Of those that a mesh axis runs over, the one named last changes fastest.
Arguments:
- vis_value: float32 [128, 128, 2, 128], P('au', 'vert'), may hold values from -6 to 6
- vis_pos: int32 [128, 128, 2, 128], P('au', 'vert'), may hold values from 0 to 1048575, as said below
- counts: int32 [128, 128], P('au', 'vert'), may hold values from 21 to 128, as said below
- kernel: float32 [8, 128], replicated, may hold values from 0.05 to 0.5
Outputs:
- image: float32 [8192, 8192], P(('au', 'vert'))
Inputs may be any that keep to these rules, and one draw needn't show every extreme that they name: Slot k of patch (p, q) holds a visibility exactly when k < counts[p, q]; in every draw some patch has all 128 slots live. vis_pos[p, q, 0, k] lies in [p * 64 * 128, (p + 1) * 64 * 128) and vis_pos[p, q, 1, k] in [q * 64 * 128, (q + 1) * 64 * 128), in every slot.
All inputs are finite; a program needn't handle non-finite values.
Results may differ from a plain program's by a relative error of at most 0.0003.
Values sent between devices are 32-bit elements; how exact they have to be, the bound alone decides.
A program may use at most 192 MiB of HBM per device.

v0:
```python
import math
import jax
import jax.numpy as jnp
from jax import lax
from jax.sharding import PartitionSpec as P

PATCH = 64
PR = 128
PC = 128
highest = lax.Precision.HIGH


def passed_along(value, axis, steps):
    count = lax.axis_size(axis)
    initial, last = (max(0, -steps), min(count, count - steps))
    return lax.ppermute(value, axis, [(source, source + steps) for source in range(initial, last)])


def fourier(length):
    index_list = jnp.arange(length, dtype=jnp.int32)
    angles = (
        2.0
        * math.pi
        / length
        * (index_list[:, None] * index_list[None, :] % length).astype(jnp.float32)
    )
    return jnp.stack([jnp.cos(angles), jnp.sin(angles)])


def twiddle(outer_size, inner_size, length):
    row_index = jnp.arange(outer_size, dtype=jnp.int32)[:, None]
    col_index = jnp.arange(inner_size, dtype=jnp.int32)[None, :]
    angles = 2.0 * math.pi / length * (row_index * col_index % length).astype(jnp.float32)
    return (jnp.cos(angles), jnp.sin(angles))


def complex_table(length):
    cos, sin = fourier(length)
    return jnp.stack([jnp.stack([cos, -sin]), jnp.stack([sin, cos])])


def row_transform(field):
    band_count, outer_size, _, rows, inner_size = field.shape
    length = outer_size * inner_size
    turn_cos, turn_sin = twiddle(outer_size, inner_size, length)
    product = jnp.einsum("scaq,bqcip->sbiap", complex_table(outer_size), field, precision=highest)
    rotated = jnp.stack(
        [
            product[0] * turn_cos - product[1] * turn_sin,
            product[0] * turn_sin + product[1] * turn_cos,
        ]
    )
    result = jnp.einsum("scyp,cbiap->sbiya", complex_table(inner_size), rotated, precision=highest)
    return result.reshape(2, band_count * rows, length)


def column_transform(received, image_scale):
    length = received.shape[1]
    item_count = received.shape[3]
    inner_size = 128
    outer_size = length // inner_size
    turn_cos, turn_sin = twiddle(outer_size, inner_size, length)
    blocked = received.reshape(2, outer_size, inner_size, item_count)
    product = jnp.einsum("scaq,cqpy->sapy", complex_table(outer_size), blocked, precision=highest)
    turn_cos = turn_cos[..., None]
    turn_sin = turn_sin[..., None]
    rotated = jnp.stack(
        [
            product[0] * turn_cos - product[1] * turn_sin,
            product[0] * turn_sin + product[1] * turn_cos,
        ]
    )
    last_table = complex_table(inner_size)[0] * image_scale
    image_rows = jnp.einsum("cbp,capy->yba", last_table, rotated, precision=highest)
    return image_rows.reshape(item_count, length)


def joined(array, group):
    count, lead, slots = array.shape
    blocks = array.reshape(count // group, group, lead, slots)
    before = jnp.roll(blocks[:, group - 1], 1, axis=0)
    return jnp.concatenate([before] + [blocks[:, step] for step in range(group)], axis=-1)


def spread(distance, taps):
    weights = jnp.zeros(distance.shape, jnp.float32)
    for tap_step in range(taps.shape[1]):
        weights = jnp.where(distance == tap_step, taps[:, tap_step][:, None], weights)
    return weights


def band_tiles(values, positions, counts, kernel):
    kernel_width, oversample = kernel.shape
    column_count, _, slot_count = values.shape
    width = 128
    group = width // PATCH
    group_count = column_count // group
    live_mask = jnp.arange(slot_count, dtype=jnp.int32)[None, :] < counts[:, None]
    cell_index = positions // oversample
    fine_index = positions - cell_index * oversample
    selector = (
        fine_index[:, :, None, :] == jnp.arange(oversample, dtype=jnp.int32)[:, None]
    ).astype(jnp.float32)
    taps = jnp.einsum("to,naok->natk", kernel, selector, precision=highest)
    taps = joined(taps.reshape(column_count, 2 * kernel_width, slot_count), group)
    cells = joined(cell_index, group)
    scaled = joined(jnp.where(live_mask[:, None], values, 0.0), group)
    extent = PATCH + kernel_width
    row_distance = (
        jnp.arange(extent, dtype=jnp.int32)[None, :, None] - (cells[:, 0] % PATCH)[:, None]
    )
    starts = jnp.arange(group_count, dtype=jnp.int32) * width
    columns = starts[:, None] + jnp.arange(width, dtype=jnp.int32)
    column_distance = columns[:, :, None] - cells[:, 1][:, None]
    row_weights = spread(row_distance, taps[:, :kernel_width])
    column_weights = spread(column_distance, taps[:, kernel_width:])
    scaled_rows = scaled[:, :, None] * row_weights[:, None]
    return jnp.einsum("mcik,mjk->mcij", scaled_rows, column_weights, precision=highest)


def local(vis_value, vis_pos, counts, kernel):
    kernel_width = kernel.shape[0]
    device_count = lax.axis_size("au") * lax.axis_size("vert")
    slot_count = vis_value.shape[3]
    image_scale = 1.0 / math.sqrt(PR * PC * slot_count)
    vert_count = lax.axis_size("vert")
    band_count = vis_value.shape[0] // vert_count
    local_columns = vis_value.shape[1]
    moved_values = lax.all_to_all(
        vis_value.reshape(vert_count, band_count, local_columns, 2, slot_count),
        "vert",
        split_axis=0,
        concat_axis=2,
        tiled=True,
    )
    positions, tallies = (
        lax.all_to_all(
            vis_pos.reshape(vert_count, band_count, local_columns, 2, slot_count),
            "vert",
            split_axis=0,
            concat_axis=2,
            tiled=True,
        ),
        lax.all_to_all(
            counts.reshape(vert_count, band_count, local_columns),
            "vert",
            split_axis=0,
            concat_axis=2,
            tiled=True,
        ),
    )
    column_count = local_columns * vert_count
    values = moved_values.reshape(band_count, column_count, 2, slot_count)
    positions = positions.reshape(band_count, column_count, 2, slot_count)
    tallies = tallies.reshape(band_count, column_count)
    tiles = lax.map(lambda members: band_tiles(*members, kernel), (values, positions, tallies))
    spill = tiles[..., PATCH:, :]
    arrived = passed_along(spill[-1], ("au", "vert"), 1)
    above = jnp.concatenate([arrived[None], spill[:-1]], axis=0)
    field = jnp.concatenate(
        [tiles[..., :kernel_width, :] + above, tiles[..., kernel_width:PATCH, :]], axis=3
    )
    row_field = row_transform(field)
    length = row_field.shape[2]
    column_share = length // device_count
    return column_transform(
        lax.all_to_all(
            row_field.reshape(2, row_field.shape[1], device_count, column_share),
            ("au", "vert"),
            split_axis=2,
            concat_axis=1,
            tiled=True,
        ),
        image_scale,
    )


def solution(mesh):
    in_specs = (P("au", "vert", None, None), P("au", "vert", None, None), P("au", "vert"), P())
    out_specs = P(("au", "vert"), None)
    return jax.shard_map(local, mesh=mesh, in_specs=in_specs, out_specs=out_specs, check_vma=False)
```

profile of v0, /device:TPU:0, one launch (start us, length us, event | category | flops | bytes accessed | tf_op | source)
XLA Modules:
  0.0 784.5 jit_solution(12170232325561670538)
XLA Ops:
  31.5 147.3 %while.12 = (s32[]{:T(128)}, f32[4,64,2,72,128]{4,1,2,3,0:T(8,128)}, s32[4,128]{1,0:T(4,128)S(1)}, f32[4,128,2,128]{3,1,2,0:T(8,128)S(1)}, s32[4,128,2,128]{3,1,2,0:T(8,128)S(1)}, /*index=5*/f32[8,128]{1,0:T(8,128)}, s32[]{:T(128)}) while((s32[]{:T(128)}, f32[4,64,2,72,128]{4,1,2,3,0:T(8,128)}, s32[4,128]{1,0:T(4,128)S(1)}, ...), condition=%wide.region_1.2_spmd, body=%wide.region_0.1_spmd.sunk | while | flops 3013378048 | bytes 48205400 | solution.py:156
  38.9 6.2 select_select_fusion.2
  46.1 18.5 %fusion.147 = f32[1,64,2,72,128]{4,3,2,1,0:T(8,128)S(1)} fusion(f32[64,384]{1,0:T(8,128)S(1)} %get-tuple-element.238, f32[64,384]{1,0:T(8,128)S(1)} %get-tuple-element.239, f32[64,384]{1,0:T(8,128)S(1)} %get-tuple-element.242, f32[64,384]{1,0:T(8,128)S(1)} %get-tuple-element.243, f32[64,384]{1,0:T(8,128)S(1)} %get-tuple-element.246, ...), kind=kOutput, calls=%fused_computation.54.clone.1 | convolution fusion | flops 2774925312 | bytes 12910592 | tf_op jit(solution)/shard_map/while/body/eval_jaxpr/mcik,mjk->mcij/dot_general | solution.py:118
  75.6 6.2 select_select_fusion.2
  82.8 18.5 %fusion.147 = f32[1,64,2,72,128]{4,3,2,1,0:T(8,128)S(1)} fusion(f32[64,384]{1,0:T(8,128)S(1)} %get-tuple-element.238, f32[64,384]{1,0:T(8,128)S(1)} %get-tuple-element.239, f32[64,384]{1,0:T(8,128)S(1)} %get-tuple-element.242, f32[64,384]{1,0:T(8,128)S(1)} %get-tuple-element.243, f32[64,384]{1,0:T(8,128)S(1)} %get-tuple-element.246, ...), kind=kOutput, calls=%fused_computation.54.clone.1 | convolution fusion | flops 2774925312 | bytes 12910592 | tf_op jit(solution)/shard_map/while/body/eval_jaxpr/mcik,mjk->mcij/dot_general | solution.py:118
  112.3 6.2 select_select_fusion.2
  119.6 18.5 %fusion.147 = f32[1,64,2,72,128]{4,3,2,1,0:T(8,128)S(1)} fusion(f32[64,384]{1,0:T(8,128)S(1)} %get-tuple-element.238, f32[64,384]{1,0:T(8,128)S(1)} %get-tuple-element.239, f32[64,384]{1,0:T(8,128)S(1)} %get-tuple-element.242, f32[64,384]{1,0:T(8,128)S(1)} %get-tuple-element.243, f32[64,384]{1,0:T(8,128)S(1)} %get-tuple-element.246, ...), kind=kOutput, calls=%fused_computation.54.clone.1 | convolution fusion | flops 2774925312 | bytes 12910592 | tf_op jit(solution)/shard_map/while/body/eval_jaxpr/mcik,mjk->mcij/dot_general | solution.py:118
  149.1 6.2 select_select_fusion.2
  156.3 18.5 %fusion.147 = f32[1,64,2,72,128]{4,3,2,1,0:T(8,128)S(1)} fusion(f32[64,384]{1,0:T(8,128)S(1)} %get-tuple-element.238, f32[64,384]{1,0:T(8,128)S(1)} %get-tuple-element.239, f32[64,384]{1,0:T(8,128)S(1)} %get-tuple-element.242, f32[64,384]{1,0:T(8,128)S(1)} %get-tuple-element.243, f32[64,384]{1,0:T(8,128)S(1)} %get-tuple-element.246, ...), kind=kOutput, calls=%fused_computation.54.clone.1 | convolution fusion | flops 2774925312 | bytes 12910592 | tf_op jit(solution)/shard_map/while/body/eval_jaxpr/mcik,mjk->mcij/dot_general | solution.py:118
  185.6 13.6 %slice.265 = f32[4,64,2,56,128]{4,1,2,3,0:T(8,128)} slice(f32[4,64,2,72,128]{4,1,2,3,0:T(8,128)} %get-tuple-element.85), slice={[0:4], [0:64], [0:2], [8:64], [0:128]} | slice | bytes 29360128 | tf_op jit(solution)/shard_map/slice | solution.py:161
  201.1 13.5 %fusion.77 = f32[2,4,64,64,128]{4,3,0,2,1:T(8,128)} fusion(f32[4,64,2,56,128]{4,1,2,3,0:T(8,128)} %slice.265, f32[4,64,2,8,128]{4,1,2,3,0:T(8,128)S(1)} %maximum_add_fusion, f32[1,2,64,64]{3,2,1,0:T(8,128)S(1)} %get-tuple-element.147, f32[1,2,64,64]{3,2,1,0:T(8,128)S(1)} %get-tuple-element.146), kind=kOutput, calls=%fused_computation.136 | convolution fusion | flops 3225436160 | bytes 33619968 | tf_op jit(solution)/shard_map/scaq,bqcip->sbiap/dot_general | solution.py:46
  214.6 9.8 %multiply_subtract_fusion.1 = (f32[1,4,64,64,128]{4,3,0,2,1:T(8,128)S(1)}, f32[1,4,64,64,128]{4,3,0,2,1:T(8,128)}) fusion(f32[2,4,64,64,128]{4,3,0,2,1:T(8,128)} %fusion.77, f32[64,128]{1,0:T(8,128)S(1)} %copy-done, f32[64,128]{1,0:T(8,128)S(1)} %copy-done.1), kind=kLoop, calls=%fused_computation.140 | loop fusion | flops 12582912 | bytes 33619968 | tf_op jit(solution)/shard_map/sub | solution.py:49
  224.4 12.7 %fusion.76 = f32[2,4,64,128,64]{3,4,0,2,1:T(8,128)} fusion(f32[1,4,64,64,128]{4,3,0,2,1:T(8,128)} %get-tuple-element.143, f32[1,4,64,64,128]{4,3,0,2,1:T(8,128)S(1)} %get-tuple-element.142, f32[1,2,128,128]{3,2,1,0:T(8,128)S(1)} %get-tuple-element.145, f32[1,2,128,128]{3,2,1,0:T(8,128)S(1)} %get-tuple-element.144), kind=kOutput, calls=%fused_computation.135 | convolution fusion | flops 6446710784 | bytes 33816576 | tf_op jit(solution)/shard_map/scyp,cbiap->sbiya/dot_general | solution.py:53
  237.1 23.0 %copy.118 = f32[2,4,64,128,64]{4,3,2,1,0:T(8,128)} copy(f32[2,4,64,128,64]{3,4,0,2,1:T(8,128)} %fusion.76) | data formatting | bytes 33554432 | tf_op jit(solution)/shard_map/scyp,cbiap->sbiya/transpose | solution.py:53
  260.1 27.9 %reshape_reshape.3 = f32[2,256,32,256]{3,2,1,0:T(8,128)} reshape(f32[2,4,64,128,64]{4,3,2,1,0:T(8,128)} %copy.118) | data formatting | bytes 33554432 | tf_op jit(solution)/shard_map/reshape;reshape | solution.py:168
  288.0 15.9 %copy.119 = f32[2,256,32,256]{3,1,0,2:T(8,128)} copy(f32[2,256,32,256]{3,2,1,0:T(8,128)} %reshape_reshape.3) | data formatting | bytes 33554432 | tf_op jit(solution)/shard_map/reshape;reshape | solution.py:168
  309.3 382.5 %all-to-all-done.3 = f32[2,256,32,256]{3,1,0,2:T(8,128)} async-done(((f32[2,256,32,256]{3,1,0,2:T(8,128)}), f32[2,256,32,256]{3,1,0,2:T(8,128)}, u32[]{:S(2)}, u32[]{:S(2)}) %all-to-all-start.3) | async-done | bytes 16777248 | tf_op jit(solution)/shard_map/all_to_all | solution.py:167
  691.8 11.5 %copy.120 = f32[2,256,32,256]{3,1,2,0:T(8,128)} copy(f32[2,256,32,256]{3,1,0,2:T(8,128)} %all-to-all-done.3) | data formatting | bytes 33554432 | tf_op jit(solution)/shard_map/all_to_all | solution.py:167
  703.3 25.6 %fusion.78 = f32[2,64,128,256]{3,1,2,0:T(8,128)} fusion(f32[2,64,128,256]{3,2,1,0:T(8,128)} %bitcast.254, f32[1,2,64,64]{3,2,1,0:T(8,128)S(1)} %get-tuple-element.147, f32[1,2,64,64]{3,2,1,0:T(8,128)S(1)} %get-tuple-element.146), kind=kOutput, calls=%fused_computation.141 | convolution fusion | flops 3221241856 | bytes 33619968 | tf_op jit(solution)/shard_map/scaq,cqpy->sapy/dot_general | solution.py:64
  728.9 13.8 %multiply_subtract_fusion = (f32[1,64,128,256]{3,1,2,0:T(8,128)}, f32[1,64,128,256]{3,1,2,0:T(8,128)}) fusion(f32[2,64,128,256]{3,1,2,0:T(8,128)} %fusion.78, f32[64,128]{0,1:T(8,128)S(1)} %copy.123, f32[64,128]{0,1:T(8,128)S(1)} %copy.122), kind=kLoop, calls=%fused_computation.138 | loop fusion | flops 12582912 | bytes 33619968 | tf_op jit(solution)/shard_map/sub | solution.py:69
  742.7 6.5 pad_maximum_fusion.2
  749.2 14.5 %fusion.81 = f32[256,128,64]{0,1,2:T(8,128)} fusion(f32[2,64,128,256]{3,1,2,0:T(8,128)S(1)} %pad_maximum_fusion.2, f32[1,128,128]{2,1,0:T(8,128)S(1)} %fusion.112, f32[1,128,128]{2,1,0:T(8,128)S(1)} %get-tuple-element.153), kind=kOutput, calls=%fused_computation.142 | convolution fusion | flops 3221291008 | bytes 25296896 | tf_op jit(solution)/shard_map/cbp,capy->yba/dot_general | solution.py:74
  763.7 11.5 %copy.125 = f32[256,128,64]{0,2,1:T(8,128)} copy(f32[256,128,64]{0,1,2:T(8,128)} %fusion.81) | data formatting | bytes 16777216 | tf_op jit(solution)/shard_map/cbp,capy->yba/transpose | solution.py:74
  775.2 8.9 %copy.126 = f32[256,8192]{1,0:T(8,128)} copy(f32[256,8192]{0,1:T(8,128)} %bitcast.258) | data formatting | bytes 16777216 | tf_op jit(solution)/shard_map/reshape | solution.py:75
  (188 shorter events, 92.4 us)
Async XLA Ops:
  1.4 9.9 %all-to-all-start = ((s32[4,1,128]{2,1,0:T(1,128)}), s32[4,1,128]{2,1,0:T(1,128)S(1)}, u32[]{:S(2)}, u32[]{:S(2)}) async-start(s32[4,1,128]{2,1,0:T(1,128)} %reshape.440), calls=%async_computation | async-start | bytes 4096 | tf_op jit(solution)/shard_map/all_to_all | solution.py:144
  11.2 10.2 %all-to-all-start.1 = ((f32[4,4,32,2,128]{4,2,3,1,0:T(8,128)}), f32[4,4,32,2,128]{4,2,3,1,0:T(8,128)S(1)}, u32[]{:S(2)}, u32[]{:S(2)}) async-start(f32[4,4,32,2,128]{4,2,3,1,0:T(8,128)} %bitcast.32), calls=%async_computation.1 | async-start | bytes 1048576 | tf_op jit(solution)/shard_map/all_to_all | solution.py:129
  21.4 10.0 %all-to-all-start.2 = ((s32[4,4,32,2,128]{4,2,3,1,0:T(8,128)}), s32[4,4,32,2,128]{4,2,3,1,0:T(8,128)S(1)}, u32[]{:S(2)}, u32[]{:S(2)}) async-start(s32[4,4,32,2,128]{4,2,3,1,0:T(8,128)} %bitcast.36), calls=%async_computation.2 | async-start | bytes 1048576 | tf_op jit(solution)/shard_map/all_to_all | solution.py:137
  31.5 152.5 %copy-start.2 = (f32[1,64,64]{2,1,0:T(8,128)S(1)}, f32[1,64,64]{2,1,0:T(8,128)}, u32[]{:S(2)}) copy-start(f32[1,64,64]{2,1,0:T(8,128)} %get-tuple-element.148) | copy-start | bytes 49156
  31.5 152.5 %copy-start.3 = (f32[1,64,64]{2,1,0:T(8,128)S(1)}, f32[1,64,64]{2,1,0:T(8,128)}, u32[]{:S(2)}) copy-start(f32[1,64,64]{2,1,0:T(8,128)} %get-tuple-element.149) | copy-start | bytes 49156
  179.9 19.3 %collective-permute-start = (f32[64,2,8,128]{3,0,1,2:T(8,128)S(1)}, f32[64,2,8,128]{3,0,1,2:T(8,128)S(1)}, u32[]{:S(2)}, u32[]{:S(2)}) collective-permute-start(f32[64,2,8,128]{3,0,1,2:T(8,128)S(1)} %slice_bitcast_fusion.7), channel_id=1, source_target_pairs={{0,1},{1,2},{2,3},{3,4},{4,5},{5,6},{6,7},{7,8},{8,9},{9,10},{10,1... | collective-permute-start | bytes 1572872 | tf_op jit(solution)/shard_map/ppermute | solution.py:16
  201.1 13.5 %copy-start = (f32[64,128]{1,0:T(8,128)S(1)}, f32[64,128]{1,0:T(8,128)}, u32[]{:S(2)}) copy-start(f32[64,128]{1,0:T(8,128)} %get-tuple-element.150) | copy-start | bytes 98308
  201.1 13.5 %copy-start.1 = (f32[64,128]{1,0:T(8,128)S(1)}, f32[64,128]{1,0:T(8,128)}, u32[]{:S(2)}) copy-start(f32[64,128]{1,0:T(8,128)} %get-tuple-element.151) | copy-start | bytes 98308
  303.9 387.9 %all-to-all-start.3 = ((f32[2,256,32,256]{3,1,0,2:T(8,128)}), f32[2,256,32,256]{3,1,0,2:T(8,128)}, u32[]{:S(2)}, u32[]{:S(2)}) async-start(f32[2,256,32,256]{3,1,0,2:T(8,128)} %copy.119), calls=%async_computation.3 | async-start | bytes 33554432 | tf_op jit(solution)/shard_map/all_to_all | solution.py:167
where the time goes:
time: 796 us; the launch traced here: 784 us
  waiting for transfers between devices  394 us (49%)
  matrix products  160 us (20%)
  local copies, waits for them, and re-layouts  145 us (18%)
  other arithmetic  63.3 us (8%)
  starting transfers between devices  20.7 us (3%)
    all_to_all x1, waiting for transfers between devices, local(): lax.all_to_all(row_field.reshape(2, row_field.shape[1], device_count, col...  382 us
    dot_general x4, matrix products, band_tiles(): jnp.einsum('mcik,mjk->mcij', scaled_rows, column_weights, precision=highest)  74.2 us
    another operation x2, local copies, waits for them, and re-layouts, local(): row_field.reshape(2, row_field.shape[1], device_count, column_share)  43.8 us
    dot_general x1, matrix products, column_transform(): jnp.einsum('scaq,cqpy->sapy', complex_table(outer_size), blocked, precisi...  25.6 us
    select_n x4, other arithmetic, spread(): jnp.where(distance == tap_step, taps[:, tap_step][:, None], weights)  24.8 us
    transpose x1, local copies, waits for them, and re-layouts, row_transform(): jnp.einsum('scyp,cbiap->sbiya', complex_table(inner_size), rotated, preci...  23 us
    dot_general x4, matrix products, band_tiles(): taps = jnp.einsum('to,naok->natk', kernel, selector, precision=highest)  19.3 us
  transfers between devices with their start and end apart: 5, of which 4 were waited for; matrix products, arithmetic and copies ran while one was open for 3% of the time, Pallas kernels for 0%

commit v1 on v0

--- a/solution.py
+++ b/solution.py
@@ -8,6 +8,15 @@
 PR = 128
 PC = 128
 highest = lax.Precision.HIGH
+seats_all_arrange = lambda local_array, join_dim, which_dim: jnp.concatenate(
+    lax.all_to_all(
+        jnp.stack(jnp.split(local_array, lax.axis_size(("au", "vert")), axis=join_dim), axis=0),
+        ("au", "vert"),
+        split_axis=0,
+        concat_axis=0,
+    ),
+    which_dim,
+)
 
 
 def passed_along(value, axis, steps):
@@ -164,12 +173,8 @@
     length = row_field.shape[2]
     column_share = length // device_count
     return column_transform(
-        lax.all_to_all(
-            row_field.reshape(2, row_field.shape[1], device_count, column_share),
-            ("au", "vert"),
-            split_axis=2,
-            concat_axis=1,
-            tiled=True,
+        seats_all_arrange(
+            row_field.reshape(2, row_field.shape[1], device_count, column_share), 2, 1
         ),
         image_scale,
     )

time: 796 us -> 892 us (1.12)
  local copies, waits for them, and re-layouts: 145 us -> 241 us
    unnamed x12 -> x43, local copies, waits for them, and re-layouts: 5.28 us -> 112 us
    another operation x2 -> x1, local copies, waits for them, and re-layouts: 43.8 us -> 28.3 us  [local(): row_field.reshape(2, row_field.shape[1], device_count, column_share)]
    reshape x0 -> x1, local copies, waits for them, and re-layouts: none -> 12.7 us  [jnp.concatenate(lax.all_to_all(jnp.stack(jnp.split(local_array, lax.axis_...]
    all_to_all x1 -> x0, local copies, waits for them, and re-layouts: 11.5 us -> none  [local(): lax.all_to_all(row_field.reshape(2, row_field.shape[1], device_count, col...]
where the time goes in v1:
time: 892 us; the launch traced here: 880 us
  waiting for transfers between devices  394 us (44%)
  local copies, waits for them, and re-layouts  241 us (27%)
  matrix products  159 us (18%)
  other arithmetic  63.5 us (7%)
  starting transfers between devices  20.6 us (2%)
    all_to_all x1, waiting for transfers between devices, lax.all_to_all(jnp.stack(jnp.split(local_array, lax.axis_size(('au', 'ver...  382 us
    unnamed x43, local copies, waits for them, and re-layouts  112 us
    dot_general x4, matrix products, band_tiles(): jnp.einsum('mcik,mjk->mcij', scaled_rows, column_weights, precision=highest)  74.2 us
    another operation x1, local copies, waits for them, and re-layouts, local(): row_field.reshape(2, row_field.shape[1], device_count, column_share)  28.3 us
    dot_general x1, matrix products, column_transform(): jnp.einsum('scaq,cqpy->sapy', complex_table(outer_size), blocked, precisi...  25.6 us
    select_n x4, other arithmetic, spread(): jnp.where(distance == tap_step, taps[:, tap_step][:, None], weights)  24.8 us
    transpose x1, local copies, waits for them, and re-layouts, row_transform(): jnp.einsum('scyp,cbiap->sbiya', complex_table(inner_size), rotated, preci...  23 us
    dot_general x4, matrix products, band_tiles(): taps = jnp.einsum('to,naok->natk', kernel, selector, precision=highest)  19.3 us
  transfers between devices with their start and end apart: 5, of which 4 were waited for; matrix products, arithmetic and copies ran while one was open for 3% of the time, Pallas kernels for 0%

profile of v1, /device:TPU:0, one launch (start us, length us, event | category | flops | bytes accessed | tf_op | source)
XLA Modules:
  0.0 879.6 jit_solution(4348975563565421045)
XLA Ops:
  1.4 5.2 all-to-all-start
  31.5 147.1 %while.12 = (s32[]{:T(128)}, f32[4,64,2,72,128]{4,1,2,3,0:T(8,128)}, s32[4,128]{1,0:T(4,128)S(1)}, f32[4,128,2,128]{3,1,2,0:T(8,128)S(1)}, s32[4,128,2,128]{3,1,2,0:T(8,128)S(1)}, /*index=5*/f32[8,128]{1,0:T(8,128)}, s32[]{:T(128)}) while((s32[]{:T(128)}, f32[4,64,2,72,128]{4,1,2,3,0:T(8,128)}, s32[4,128]{1,0:T(4,128)S(1)}, ...), condition=%wide.region_1.2_spmd, body=%wide.region_0.1_spmd.sunk | while | flops 3013378048 | bytes 48205400 | solution.py:165
  38.9 6.2 select_select_fusion.2
  46.1 18.5 %fusion.179 = f32[1,64,2,72,128]{4,3,2,1,0:T(8,128)S(1)} fusion(f32[64,384]{1,0:T(8,128)S(1)} %get-tuple-element.238, f32[64,384]{1,0:T(8,128)S(1)} %get-tuple-element.239, f32[64,384]{1,0:T(8,128)S(1)} %get-tuple-element.242, f32[64,384]{1,0:T(8,128)S(1)} %get-tuple-element.243, f32[64,384]{1,0:T(8,128)S(1)} %get-tuple-element.246, ...), kind=kOutput, calls=%fused_computation.54.clone.1 | convolution fusion | flops 2774925312 | bytes 12910592 | tf_op jit(solution)/shard_map/while/body/eval_jaxpr/mcik,mjk->mcij/dot_general | solution.py:127
  75.6 6.2 select_select_fusion.2
  82.8 18.5 %fusion.179 = f32[1,64,2,72,128]{4,3,2,1,0:T(8,128)S(1)} fusion(f32[64,384]{1,0:T(8,128)S(1)} %get-tuple-element.238, f32[64,384]{1,0:T(8,128)S(1)} %get-tuple-element.239, f32[64,384]{1,0:T(8,128)S(1)} %get-tuple-element.242, f32[64,384]{1,0:T(8,128)S(1)} %get-tuple-element.243, f32[64,384]{1,0:T(8,128)S(1)} %get-tuple-element.246, ...), kind=kOutput, calls=%fused_computation.54.clone.1 | convolution fusion | flops 2774925312 | bytes 12910592 | tf_op jit(solution)/shard_map/while/body/eval_jaxpr/mcik,mjk->mcij/dot_general | solution.py:127
  112.3 6.2 select_select_fusion.2
  119.6 18.5 %fusion.179 = f32[1,64,2,72,128]{4,3,2,1,0:T(8,128)S(1)} fusion(f32[64,384]{1,0:T(8,128)S(1)} %get-tuple-element.238, f32[64,384]{1,0:T(8,128)S(1)} %get-tuple-element.239, f32[64,384]{1,0:T(8,128)S(1)} %get-tuple-element.242, f32[64,384]{1,0:T(8,128)S(1)} %get-tuple-element.243, f32[64,384]{1,0:T(8,128)S(1)} %get-tuple-element.246, ...), kind=kOutput, calls=%fused_computation.54.clone.1 | convolution fusion | flops 2774925312 | bytes 12910592 | tf_op jit(solution)/shard_map/while/body/eval_jaxpr/mcik,mjk->mcij/dot_general | solution.py:127
  149.1 6.2 select_select_fusion.2
  156.3 18.5 %fusion.179 = f32[1,64,2,72,128]{4,3,2,1,0:T(8,128)S(1)} fusion(f32[64,384]{1,0:T(8,128)S(1)} %get-tuple-element.238, f32[64,384]{1,0:T(8,128)S(1)} %get-tuple-element.239, f32[64,384]{1,0:T(8,128)S(1)} %get-tuple-element.242, f32[64,384]{1,0:T(8,128)S(1)} %get-tuple-element.243, f32[64,384]{1,0:T(8,128)S(1)} %get-tuple-element.246, ...), kind=kOutput, calls=%fused_computation.54.clone.1 | convolution fusion | flops 2774925312 | bytes 12910592 | tf_op jit(solution)/shard_map/while/body/eval_jaxpr/mcik,mjk->mcij/dot_general | solution.py:127
  185.4 13.6 %slice.265 = f32[4,64,2,56,128]{4,1,2,3,0:T(8,128)} slice(f32[4,64,2,72,128]{4,1,2,3,0:T(8,128)} %get-tuple-element.85), slice={[0:4], [0:64], [0:2], [8:64], [0:128]} | slice | bytes 29360128 | tf_op jit(solution)/shard_map/slice | solution.py:170
  201.0 13.5 %fusion.77 = f32[2,4,64,64,128]{4,3,0,2,1:T(8,128)} fusion(f32[4,64,2,56,128]{4,1,2,3,0:T(8,128)} %slice.265, f32[4,64,2,8,128]{4,1,2,3,0:T(8,128)S(1)} %maximum_add_fusion, f32[1,2,64,64]{3,2,1,0:T(8,128)S(1)} %get-tuple-element.147, f32[1,2,64,64]{3,2,1,0:T(8,128)S(1)} %get-tuple-element.146), kind=kOutput, calls=%fused_computation.136 | convolution fusion | flops 3225436160 | bytes 33619968 | tf_op jit(solution)/shard_map/scaq,bqcip->sbiap/dot_general | solution.py:55
  214.5 9.8 %multiply_subtract_fusion.1 = (f32[1,4,64,64,128]{4,3,0,2,1:T(8,128)S(1)}, f32[1,4,64,64,128]{4,3,0,2,1:T(8,128)}) fusion(f32[2,4,64,64,128]{4,3,0,2,1:T(8,128)} %fusion.77, f32[64,128]{1,0:T(8,128)S(1)} %copy-done, f32[64,128]{1,0:T(8,128)S(1)} %copy-done.1), kind=kLoop, calls=%fused_computation.140 | loop fusion | flops 12582912 | bytes 33619968 | tf_op jit(solution)/shard_map/sub | solution.py:58
  224.3 12.7 %fusion.76 = f32[2,4,64,128,64]{3,4,0,2,1:T(8,128)} fusion(f32[1,4,64,64,128]{4,3,0,2,1:T(8,128)} %get-tuple-element.143, f32[1,4,64,64,128]{4,3,0,2,1:T(8,128)S(1)} %get-tuple-element.142, f32[1,2,128,128]{3,2,1,0:T(8,128)S(1)} %get-tuple-element.145, f32[1,2,128,128]{3,2,1,0:T(8,128)S(1)} %get-tuple-element.144), kind=kOutput, calls=%fused_computation.135 | convolution fusion | flops 6446710784 | bytes 33816576 | tf_op jit(solution)/shard_map/scyp,cbiap->sbiya/dot_general | solution.py:62
  236.9 23.0 %copy.117 = f32[2,4,64,128,64]{4,3,2,1,0:T(8,128)} copy(f32[2,4,64,128,64]{3,4,0,2,1:T(8,128)} %fusion.76) | data formatting | bytes 33554432 | tf_op jit(solution)/shard_map/scyp,cbiap->sbiya/transpose | solution.py:62
  259.9 28.3 %reshape_reshape.6 = f32[2,256,32,256]{3,2,1,0:T(8,128)} reshape(f32[2,4,64,128,64]{4,3,2,1,0:T(8,128)} %copy.117) | data formatting | bytes 33554432 | tf_op jit(solution)/shard_map/reshape;reshape | solution.py:177
  403.2 382.5 %all-to-all-done.3 = f32[32,2,256,1,256]{4,3,2,1,0:T(1,128)} async-done(((f32[32,2,256,1,256]{4,3,2,1,0:T(1,128)}), f32[32,2,256,1,256]{4,3,2,1,0:T(1,128)}, u32[]{:S(2)}, u32[]{:S(2)}) %all-to-all-start.3) | async-done | bytes 16777248 | tf_op jit(solution)/shard_map/all_to_all | solution.py:12
  785.7 12.7 %copy.118 = f32[2,32,256,1,256]{4,2,1,0,3:T(8,128)} copy(f32[2,32,256,1,256]{4,3,2,0,1:T(1,128)} %bitcast.91) | data formatting | bytes 33554432 | tf_op jit(solution)/shard_map/reshape | solution.py:11
  798.4 25.6 %fusion.78 = f32[2,64,128,256]{3,1,2,0:T(8,128)} fusion(f32[2,64,128,256]{3,2,1,0:T(8,128)} %bitcast.379, f32[1,2,64,64]{3,2,1,0:T(8,128)S(1)} %get-tuple-element.147, f32[1,2,64,64]{3,2,1,0:T(8,128)S(1)} %get-tuple-element.146), kind=kOutput, calls=%fused_computation.141 | convolution fusion | flops 3221241856 | bytes 33619968 | tf_op jit(solution)/shard_map/scaq,cqpy->sapy/dot_general | solution.py:73
  824.0 13.8 %multiply_subtract_fusion = (f32[1,64,128,256]{3,1,2,0:T(8,128)}, f32[1,64,128,256]{3,1,2,0:T(8,128)}) fusion(f32[2,64,128,256]{3,1,2,0:T(8,128)} %fusion.78, f32[64,128]{0,1:T(8,128)S(1)} %copy.121, f32[64,128]{0,1:T(8,128)S(1)} %copy.120), kind=kLoop, calls=%fused_computation.138 | loop fusion | flops 12582912 | bytes 33619968 | tf_op jit(solution)/shard_map/sub | solution.py:78
  837.8 6.7 pad_maximum_fusion.2
  844.5 14.3 %fusion.81 = f32[256,128,64]{0,1,2:T(8,128)} fusion(f32[2,64,128,256]{3,1,2,0:T(8,128)S(1)} %pad_maximum_fusion.2, f32[1,128,128]{2,1,0:T(8,128)S(1)} %fusion.144, f32[1,128,128]{2,1,0:T(8,128)S(1)} %get-tuple-element.153), kind=kOutput, calls=%fused_computation.142 | convolution fusion | flops 3221291008 | bytes 25296896 | tf_op jit(solution)/shard_map/cbp,capy->yba/dot_general | solution.py:83
  858.8 11.5 %copy.123 = f32[256,128,64]{0,2,1:T(8,128)} copy(f32[256,128,64]{0,1,2:T(8,128)} %fusion.81) | data formatting | bytes 16777216 | tf_op jit(solution)/shard_map/cbp,capy->yba/transpose | solution.py:83
  870.3 8.9 %copy.124 = f32[256,8192]{1,0:T(8,128)} copy(f32[256,8192]{0,1:T(8,128)} %bitcast.383) | data formatting | bytes 16777216 | tf_op jit(solution)/shard_map/reshape | solution.py:84
  (219 shorter events, 196.8 us)
Async XLA Ops:
  1.4 9.9 %all-to-all-start = ((s32[4,1,128]{2,1,0:T(1,128)}), s32[4,1,128]{2,1,0:T(1,128)S(1)}, u32[]{:S(2)}, u32[]{:S(2)}) async-start(s32[4,1,128]{2,1,0:T(1,128)} %reshape.439), calls=%async_computation | async-start | bytes 4096 | tf_op jit(solution)/shard_map/all_to_all | solution.py:153
  11.2 10.2 %all-to-all-start.1 = ((f32[4,4,32,2,128]{4,2,3,1,0:T(8,128)}), f32[4,4,32,2,128]{4,2,3,1,0:T(8,128)S(1)}, u32[]{:S(2)}, u32[]{:S(2)}) async-start(f32[4,4,32,2,128]{4,2,3,1,0:T(8,128)} %bitcast.32), calls=%async_computation.1 | async-start | bytes 1048576 | tf_op jit(solution)/shard_map/all_to_all | solution.py:138
  21.4 10.0 %all-to-all-start.2 = ((s32[4,4,32,2,128]{4,2,3,1,0:T(8,128)}), s32[4,4,32,2,128]{4,2,3,1,0:T(8,128)S(1)}, u32[]{:S(2)}, u32[]{:S(2)}) async-start(s32[4,4,32,2,128]{4,2,3,1,0:T(8,128)} %bitcast.36), calls=%async_computation.2 | async-start | bytes 1048576 | tf_op jit(solution)/shard_map/all_to_all | solution.py:146
  31.5 152.3 %copy-start.2 = (f32[1,64,64]{2,1,0:T(8,128)S(1)}, f32[1,64,64]{2,1,0:T(8,128)}, u32[]{:S(2)}) copy-start(f32[1,64,64]{2,1,0:T(8,128)} %get-tuple-element.148) | copy-start | bytes 49156
  31.5 152.3 %copy-start.3 = (f32[1,64,64]{2,1,0:T(8,128)S(1)}, f32[1,64,64]{2,1,0:T(8,128)}, u32[]{:S(2)}) copy-start(f32[1,64,64]{2,1,0:T(8,128)} %get-tuple-element.149) | copy-start | bytes 49156
  179.7 19.3 %collective-permute-start = (f32[64,2,8,128]{3,0,1,2:T(8,128)S(1)}, f32[64,2,8,128]{3,0,1,2:T(8,128)S(1)}, u32[]{:S(2)}, u32[]{:S(2)}) collective-permute-start(f32[64,2,8,128]{3,0,1,2:T(8,128)S(1)} %slice_bitcast_fusion.39), channel_id=1, source_target_pairs={{0,1},{1,2},{2,3},{3,4},{4,5},{5,6},{6,7},{7,8},{8,9},{9,10},{10,1... | collective-permute-start | bytes 1572872 | tf_op jit(solution)/shard_map/ppermute | solution.py:25
  201.0 13.5 %copy-start = (f32[64,128]{1,0:T(8,128)S(1)}, f32[64,128]{1,0:T(8,128)}, u32[]{:S(2)}) copy-start(f32[64,128]{1,0:T(8,128)} %get-tuple-element.150) | copy-start | bytes 98308
  201.0 13.5 %copy-start.1 = (f32[64,128]{1,0:T(8,128)S(1)}, f32[64,128]{1,0:T(8,128)}, u32[]{:S(2)}) copy-start(f32[64,128]{1,0:T(8,128)} %get-tuple-element.151) | copy-start | bytes 98308
  398.0 387.7 %all-to-all-start.3 = ((f32[32,2,256,1,256]{4,3,2,1,0:T(1,128)}), f32[32,2,256,1,256]{4,3,2,1,0:T(1,128)}, u32[]{:S(2)}, u32[]{:S(2)}) async-start(f32[32,2,256,1,256]{4,3,2,1,0:T(1,128)} %fusion.84), calls=%async_computation.3 | async-start | bytes 33554432 | tf_op jit(solution)/shard_map/all_to_all | solution.py:12
